TPU v7x, 32 devices: a whole 2x2x4 slice. The times are simulated.
32 devices in a mesh: dp: 8 (over z, y), tensor: 4 (over x, core).
Axes of the slice: x: 2, y: 2, z: 4, core: 2. Of those that a mesh axis runs over, the one named last changes fastest.
Arguments:
- tokens: bfloat16 [2048, 2048], P('dp'), may hold values from -6 to 6
- documents: int32 [8, 256], P('dp'), may hold values from 0 to 7, never falling along the last dimension, each value on 1 to 128 neighbouring positions
- cotangent: bfloat16 [2048, 2048], P('dp'), may hold values from -6 to 6
- qkv_weight: float32 [3, 2048, 2048], P(None, 'dp', 'tensor'), may hold values from -0.1875 to 0.1875
- out_weight: float32 [2048, 2048], P(('tensor', 'dp')), may hold values from -0.25 to 0.25
- lift_weight: float32 [2, 2048, 8192], P(None, 'dp', 'tensor'), may hold values from -0.125 to 0.125
- down_weight: float32 [8192, 2048], P(('tensor', 'dp')), may hold values from -0.0625 to 0.0625
- gains: float32 [2, 2048], P(None, 'dp'), may hold values from 0.5 to 1.5
- qkv_first: float32 [3, 2048, 2048], P(None, 'dp', 'tensor'), may hold values from -3.5 to 3.5
- out_first: float32 [2048, 2048], P(('tensor', 'dp')), may hold values from -3.5 to 3.5
- lift_first: float32 [2, 2048, 8192], P(None, 'dp', 'tensor'), may hold values from -3.5 to 3.5
- down_first: float32 [8192, 2048], P(('tensor', 'dp')), may hold values from -3.5 to 3.5
- gains_first: float32 [2, 2048], P(None, 'dp'), may hold values from -3.5 to 3.5
- qkv_second: float32 [3, 2048, 2048], P(None, 'dp', 'tensor'), may hold values from 0.21038716 to 0.8415486
- out_second: float32 [2048, 2048], P(('tensor', 'dp')), may hold values from 0.21038716 to 0.8415486
- lift_second: float32 [2, 2048, 8192], P(None, 'dp', 'tensor'), may hold values from 0.21038716 to 0.8415486
- down_second: float32 [8192, 2048], P(('tensor', 'dp')), may hold values from 0.21038716 to 0.8415486
- gains_second: float32 [2, 2048], P(None, 'dp'), may hold values from 0.21038716 to 0.8415486
Outputs:
- layer_out: bfloat16 [2048, 2048], P('dp')
- grad_tokens: float32 [2048, 2048], P('dp')
- qkv_new: float32 [3, 2048, 2048], P(None, 'dp', 'tensor')
- out_new: float32 [2048, 2048], P(('tensor', 'dp'))
- lift_new: float32 [2, 2048, 8192], P(None, 'dp', 'tensor')
- down_new: float32 [8192, 2048], P(('tensor', 'dp'))
- gains_new: float32 [2, 2048], P(None, 'dp')
- qkv_moment: float32 [3, 2048, 2048], P(None, 'dp', 'tensor')
- out_moment: float32 [2048, 2048], P(('tensor', 'dp'))
- lift_moment: float32 [2, 2048, 8192], P(None, 'dp', 'tensor')
- down_moment: float32 [8192, 2048], P(('tensor', 'dp'))
- gains_moment: float32 [2, 2048], P(None, 'dp')
- qkv_variance: float32 [3, 2048, 2048], P(None, 'dp', 'tensor')
- out_variance: float32 [2048, 2048], P(('tensor', 'dp'))
- lift_variance: float32 [2, 2048, 8192], P(None, 'dp', 'tensor')
- down_variance: float32 [8192, 2048], P(('tensor', 'dp'))
- gains_variance: float32 [2, 2048], P(None, 'dp')
- grad_norm: float32 [], replicated
Inputs may be any that keep to these rules, and one draw needn't show every extreme that they name: Each row of documents is one sequence: ids never fall along the row, and each id is one document of 1 to 128 tokens.
All inputs are finite; a program needn't handle non-finite values.
Results may differ from a plain program's by a relative error of at most 0.015.
The roundings to bfloat16 on the way count: a program that leaves them out, or rounds other values in their place, can miss the bound.
Values may be sent and summed in bfloat16 or wider, within the bound.
No kernel may reach another device: no remote copies, remote signals or barrier semaphores. Data moves between devices by JAX's collectives and lax.ppermute only.
A program may use at most 256 MiB of HBM per device.

v0:
```python
import math

import jax
import jax.numpy as jnp
from jax import lax
from jax.sharding import PartitionSpec as P

HD = 128
STEP = 10
CLIP_NORM = 16384


norm_eps = 1e-05
beta_one = 0.9
beta_two = 0.95
adam_eps = 1e-08
rate_matrix = 0.02
rate_gain = 0.5
decay_matrix = 0.1


def norm_forward(rows, gain):
    inverse = lax.rsqrt(jnp.mean(rows * rows, axis=-1, keepdims=True) + norm_eps)
    scaled = rows * inverse
    return (scaled, inverse, (scaled * gain).astype(jnp.bfloat16))


def norm_backward(incoming, scaled, inverse, gain):
    grad_gain = jnp.sum(incoming * scaled, axis=0)
    weighted = incoming * gain
    grad_rows = inverse * (weighted - scaled * jnp.mean(weighted * scaled, axis=-1, keepdims=True))
    return (grad_gain, grad_rows)


def block_probs(queries, keys, doc_row, start, block, scale, offset):
    length = keys.shape[0]
    query_pos = start + jnp.arange(block, dtype=jnp.int32)
    key_pos = jnp.arange(length, dtype=jnp.int32)
    allowed = (query_pos[:, None] >= key_pos[None, :]) & (doc_row[:, None] == doc_row[None, :])
    scores = (
        jnp.einsum("qhd,khd->hqk", queries, keys, preferred_element_type=jnp.float32) * scale
        + offset
    )
    probs = jnp.where(allowed[None], jax.nn.sigmoid(scores), 0.0)
    return (queries, probs)


def adam_step(weight, first, second, grad, factor, rate, decay):
    clipped = grad * factor
    moment = beta_one * first + (1.0 - beta_one) * clipped
    variance = beta_two * second + (1.0 - beta_two) * clipped * clipped
    corr_one = 1.0 - beta_one**STEP
    corr_two = 1.0 - beta_two**STEP
    update = moment / corr_one / (jnp.sqrt(variance / corr_two) + adam_eps)
    return (weight - rate * (update + decay * weight), moment, variance)


def on_device(
    tokens,
    documents,
    cotangent,
    qkv_weight,
    out_weight,
    lift_weight,
    down_weight,
    gains,
    qkv_first,
    out_first,
    lift_first,
    down_first,
    gains_first,
    qkv_second,
    out_second,
    lift_second,
    down_second,
    gains_second,
):
    bf16 = jnp.bfloat16
    f32 = jnp.float32
    w_qkv, w_out, w_lift, w_down, w_gains = (
        lax.all_gather(qkv_weight.astype(bf16), "dp", axis=1, tiled=True),
        lax.all_gather(out_weight.astype(bf16), "dp", axis=0, tiled=True),
        lax.all_gather(lift_weight.astype(bf16), "dp", axis=1, tiled=True),
        lax.all_gather(down_weight.astype(bf16), "dp", axis=0, tiled=True),
        lax.all_gather(gains.astype(bf16), "dp", axis=1, tiled=True),
    )
    length = tokens.shape[0]
    local_width = w_qkv.shape[2]
    heads = local_width // HD
    block = min(512, length)
    blocks = length // block
    scale = 1.0 / math.sqrt(HD)
    offset = -math.log(length)
    doc_row = documents[0]
    gain_one = w_gains[0].astype(f32)
    gain_two = w_gains[1].astype(f32)
    x_rows = tokens.astype(f32)
    scaled_one, inverse_one, normed_one = norm_forward(x_rows, gain_one)
    project = jnp.einsum("td,cde->cte", normed_one, w_qkv, preferred_element_type=f32).astype(bf16)
    queries = project[0].reshape(length, heads, HD)
    keys = project[1].reshape(length, heads, HD)
    values = project[2].reshape(length, heads, HD)

    def attend(index):
        start = index * block
        query_block, probs = block_probs(queries, keys, doc_row, start, block, scale, offset)
        return jnp.einsum(
            "hqk,khd->qhd", probs.astype(bf16), values, preferred_element_type=f32
        ).astype(bf16)

    attended = lax.map(attend, jnp.arange(blocks, dtype=jnp.int32)).reshape(length, local_width)
    branch = lax.psum(jnp.dot(attended, w_out, preferred_element_type=f32), "tensor")
    middle = x_rows + branch
    scaled_two, inverse_two, normed_two = norm_forward(middle, gain_two)
    gate_up = jnp.einsum("td,cde->cte", normed_two, w_lift, preferred_element_type=f32)
    gate = gate_up[0]
    upward = gate_up[1]
    sigma = jax.nn.sigmoid(gate)
    hidden = (gate * sigma * upward).astype(bf16)
    feed = lax.psum(
        jnp.dot(hidden, w_down, preferred_element_type=f32).astype(jnp.bfloat16), "tensor"
    ).astype(jnp.float32)
    layer_out = (middle + feed).astype(bf16)
    grad_incoming = cotangent.astype(f32)
    grad_down = jnp.einsum("tf,td->fd", hidden, cotangent, preferred_element_type=f32)
    grad_hidden = jnp.einsum("td,fd->tf", cotangent, w_down, preferred_element_type=f32)
    grad_gate = (grad_hidden * upward * sigma * (1.0 + gate * (1.0 - sigma))).astype(bf16)
    grad_up = (grad_hidden * gate * sigma).astype(bf16)
    grad_pair = jnp.stack([grad_gate, grad_up])
    grad_lift = jnp.einsum("td,ctf->cdf", normed_two, grad_pair, preferred_element_type=f32)
    back_two = lax.psum(
        jnp.einsum("ctf,cdf->td", grad_pair, w_lift, preferred_element_type=f32), "tensor"
    )
    grad_gain_two, grad_mid_norm = norm_backward(back_two, scaled_two, inverse_two, gain_two)
    grad_mid = grad_incoming + grad_mid_norm
    grad_branch = grad_mid.astype(bf16)
    grad_out = jnp.einsum("te,td->ed", attended, grad_branch, preferred_element_type=f32)
    grad_attended = jnp.einsum("td,ed->te", grad_branch, w_out, preferred_element_type=f32).astype(
        bf16
    )
    grad_heads = grad_attended.reshape(length, heads, HD)

    def attend_back(carry, index):
        grad_keys, grad_values = carry
        start = index * block
        query_block, probs = block_probs(queries, keys, doc_row, start, block, scale, offset)
        grad_probs = jnp.einsum("qhd,khd->hqk", grad_heads, values, preferred_element_type=f32)
        grad_scores = (grad_probs * probs * (1.0 - probs)).astype(bf16)
        grad_query = (
            jnp.einsum("hqk,khd->qhd", grad_scores, keys, preferred_element_type=f32) * scale
        )
        grad_keys = (
            grad_keys
            + jnp.einsum("hqk,qhd->khd", grad_scores, query_block, preferred_element_type=f32)
            * scale
        )
        grad_values = grad_values + jnp.einsum(
            "hqk,qhd->khd", probs.astype(bf16), grad_heads, preferred_element_type=f32
        )
        return ((grad_keys, grad_values), grad_query)

    zeros_kv = jnp.zeros((length, heads, HD), f32)
    (grad_keys, grad_values), grad_queries = lax.scan(
        attend_back, (zeros_kv, zeros_kv), jnp.arange(blocks, dtype=jnp.int32)
    )
    grad_project = jnp.stack(
        [
            grad_queries.reshape(length, local_width),
            grad_keys.reshape(length, local_width),
            grad_values.reshape(length, local_width),
        ]
    ).astype(bf16)
    grad_qkv = jnp.einsum("td,cte->cde", normed_one, grad_project, preferred_element_type=f32)
    back_one = lax.psum(
        jnp.einsum("cte,cde->td", grad_project, w_qkv, preferred_element_type=f32), "tensor"
    )
    grad_gain_one, grad_x_norm = norm_backward(back_one, scaled_one, inverse_one, gain_one)
    grad_tokens = grad_mid + grad_x_norm
    grad_gains = jnp.stack([grad_gain_one, grad_gain_two])
    red_qkv, red_out, red_lift, red_down, red_gains = (
        lax.psum_scatter(grad_qkv, "dp", scatter_dimension=1, tiled=True),
        lax.psum_scatter(grad_out, "dp", scatter_dimension=0, tiled=True),
        lax.psum_scatter(grad_lift, "dp", scatter_dimension=1, tiled=True),
        lax.psum_scatter(grad_down, "dp", scatter_dimension=0, tiled=True),
        lax.psum_scatter(grad_gains, "dp", scatter_dimension=1, tiled=True),
    )
    local_total = (
        jnp.sum(red_qkv * red_qkv)
        + jnp.sum(red_out * red_out)
        + jnp.sum(red_lift * red_lift)
        + jnp.sum(red_down * red_down)
        + jnp.sum(red_gains * red_gains) / lax.axis_size("tensor")
    )
    total = lax.psum(local_total, ("dp", "tensor"))
    grad_norm = jnp.sqrt(total)
    factor = CLIP_NORM / jnp.maximum(grad_norm, CLIP_NORM)
    qkv_new, qkv_moment, qkv_variance = adam_step(
        qkv_weight, qkv_first, qkv_second, red_qkv, factor, rate_matrix, decay_matrix
    )
    out_new, out_moment, out_variance = adam_step(
        out_weight, out_first, out_second, red_out, factor, rate_matrix, decay_matrix
    )
    lift_new, lift_moment, lift_variance = adam_step(
        lift_weight, lift_first, lift_second, red_lift, factor, rate_matrix, decay_matrix
    )
    down_new, down_moment, down_variance = adam_step(
        down_weight, down_first, down_second, red_down, factor, rate_matrix, decay_matrix
    )
    gains_new, gains_moment, gains_variance = adam_step(
        gains, gains_first, gains_second, red_gains, factor, rate_gain, 0.0
    )
    return (
        layer_out,
        grad_tokens,
        qkv_new,
        out_new,
        lift_new,
        down_new,
        gains_new,
        qkv_moment,
        out_moment,
        lift_moment,
        down_moment,
        gains_moment,
        qkv_variance,
        out_variance,
        lift_variance,
        down_variance,
        gains_variance,
        grad_norm,
    )


def solution(mesh):
    placed = (
        P("dp", None),
        P("dp", None),
        P("dp", None),
        P(None, "dp", "tensor"),
        P(("tensor", "dp"), None),
        P(None, "dp", "tensor"),
        P(("tensor", "dp"), None),
        P(None, "dp"),
        P(None, "dp", "tensor"),
        P(("tensor", "dp"), None),
        P(None, "dp", "tensor"),
        P(("tensor", "dp"), None),
        P(None, "dp"),
        P(None, "dp", "tensor"),
        P(("tensor", "dp"), None),
        P(None, "dp", "tensor"),
        P(("tensor", "dp"), None),
        P(None, "dp"),
    )
    return jax.shard_map(
        on_device,
        mesh=mesh,
        in_specs=placed,
        out_specs=(
            P("dp", None),
            P("dp", None),
            P(None, "dp", "tensor"),
            P(("tensor", "dp"), None),
            P(None, "dp", "tensor"),
            P(("tensor", "dp"), None),
            P(None, "dp"),
            P(None, "dp", "tensor"),
            P(("tensor", "dp"), None),
            P(None, "dp", "tensor"),
            P(("tensor", "dp"), None),
            P(None, "dp"),
            P(None, "dp", "tensor"),
            P(("tensor", "dp"), None),
            P(None, "dp", "tensor"),
            P(("tensor", "dp"), None),
            P(None, "dp"),
            P(),
        ),
        check_vma=False,
    )
```

profile of v0, /device:TPU:0, one launch (start us, length us, event | category | flops | bytes accessed | tf_op | source)
XLA Modules:
  0.0 2062.5 jit_solution(4781406800349877402)
XLA Ops:
  10.7 22.7 %all_gather.15 = bf16[2,2048]{1,0:T(2,128)(2,1)S(1)} all-gather(bf16[2,256]{1,0:T(2,128)(2,1)S(1)} %convert_element_type.80), channel_id=1, replica_groups=mesh['dp'=8,'tensor'=4] {'dp'}, dimensions={1}, use_global_device_ids=true | all-gather | bytes 9216 | tf_op jit(solution)/shard_map/all_gather | solution.py:85
  33.8 78.4 %all-gather.5.cloned.1.call-done = bf16[3,2048,512]{2,1,0:T(8,128)(2,1)} async-done(((bf16[3,256,512]{2,1,0:T(8,128)(2,1)}), bf16[3,2048,512]{2,1,0:T(8,128)(2,1)}) %all-gather.5.cloned.1.call-update) | async-done | bytes 6291472 | tf_op jit(solution)/shard_map/all_gather | solution.py:81
  119.3 42.9 %all-gather.7.cloned.1.call-done = bf16[512,2048]{1,0:T(8,128)(2,1)} async-done(((bf16[64,2048]{1,0:T(8,128)(2,1)}), bf16[512,2048]{1,0:T(8,128)(2,1)}) %all-gather.7.cloned.1.call-update) | async-done | bytes 2097168 | tf_op jit(solution)/shard_map/all_gather | solution.py:82
  173.2 42.8 %all-reduce.5.cloned.1.call-done = f32[256,2048]{1,0:T(8,128)} async-done(((f32[256,2048]{1,0:T(8,128)}), f32[256,2048]{1,0:T(8,128)}) %all-reduce.5.cloned.1.call-update) | async-done | bytes 2097168 | tf_op jit(solution)/shard_map/psum | solution.py:112
  218.0 228.0 %all-gather.9.cloned.1.call-done = bf16[2,2048,2048]{2,1,0:T(8,128)(2,1)} async-done(((bf16[2,256,2048]{2,1,0:T(8,128)(2,1)}), bf16[2,2048,2048]{2,1,0:T(8,128)(2,1)}) %all-gather.9.cloned.1.call-update) | async-done | bytes 16777232 | tf_op jit(solution)/shard_map/all_gather | solution.py:83
  446.0 10.2 convolution_bitcast_fusion.2
  456.2 115.0 %all-gather.11.cloned.1.call-done = bf16[2048,2048]{1,0:T(8,128)(2,1)} async-done(((bf16[256,2048]{1,0:T(8,128)(2,1)}), bf16[2048,2048]{1,0:T(8,128)(2,1)}) %all-gather.11.cloned.1.call-update) | async-done | bytes 8388624 | tf_op jit(solution)/shard_map/all_gather | solution.py:84
  571.2 9.7 fusion.28
  580.9 12.3 convolution_bitcast_fusion.4
  593.2 7.1 convolution_convert_fusion
  600.5 42.4 %all-reduce.9.cloned.1.call-done = f32[256,2048]{1,0:T(8,128)} async-done(((f32[256,2048]{1,0:T(8,128)}), f32[256,2048]{1,0:T(8,128)}) %all-reduce.9.cloned.1.call-update) | async-done | bytes 2097168 | tf_op jit(solution)/shard_map/psum | solution.py:131
  645.1 37.2 %all-reduce.7.cloned.1.call-done = bf16[256,2048]{1,0:T(8,128)(2,1)} async-done(((bf16[256,2048]{1,0:T(8,128)(2,1)}), bf16[256,2048]{1,0:T(8,128)(2,1)}) %all-reduce.7.cloned.1.call-update) | async-done | bytes 1048592 | tf_op jit(solution)/shard_map/psum | solution.py:120
  701.9 6.2 convolution_bitcast_fusion.3
  708.2 52.0 %all-reduce.11.cloned.1.call-done = f32[256,2048]{1,0:T(8,128)} async-done(((f32[256,2048]{1,0:T(8,128)}), f32[256,2048]{1,0:T(8,128)}) %all-reduce.11.cloned.1.call-update) | async-done | bytes 2097168 | tf_op jit(solution)/shard_map/psum | solution.py:174
  769.1 7.5 convolution_bitcast_fusion.1
  776.6 9.7 fusion.54
  786.6 15.0 convolution_bitcast_fusion
  830.6 89.2 %reduce-scatter.10.cloned.1.call-done = f32[64,2048]{1,0:T(8,128)} async-done(((f32[512,2048]{1,0:T(8,128)}), f32[64,2048]{1,0:T(8,128)}) %reduce-scatter.10.cloned.1.call-update) | async-done | bytes 524304 | tf_op jit(solution)/shard_map/reduce_scatter | solution.py:182
  921.6 209.4 %reduce-scatter.8.cloned.1.call-done = f32[3,256,512]{1,2,0:T(8,128)} async-done(((f32[3,2048,512]{1,2,0:T(8,128)}), f32[3,256,512]{1,2,0:T(8,128)}) %reduce-scatter.8.cloned.1.call-update) | async-done | bytes 1572880 | tf_op jit(solution)/shard_map/reduce_scatter | solution.py:181
  1134.7 279.3 %reduce-scatter.14.cloned.1.call-done = f32[256,2048]{1,0:T(8,128)} async-done(((f32[2048,2048]{1,0:T(8,128)}), f32[256,2048]{1,0:T(8,128)}) %reduce-scatter.14.cloned.1.call-update) | async-done | bytes 2097168 | tf_op jit(solution)/shard_map/reduce_scatter | solution.py:184
  1416.7 538.7 %reduce-scatter.12.cloned.1.call-done = f32[2,256,2048]{1,2,0:T(8,128)} async-done(((f32[2,2048,2048]{1,2,0:T(8,128)}), f32[2,256,2048]{1,2,0:T(8,128)}) %reduce-scatter.12.cloned.1.call-update) | async-done | bytes 4194320 | tf_op jit(solution)/shard_map/reduce_scatter | solution.py:183
  1964.1 39.5 %psum.39 = f32[]{:T(128)} all-reduce(f32[]{:T(128)S(6)} %add.183), channel_id=1, replica_groups=mesh['dp'=8,'tensor'=4] {'dp','tensor'}, use_global_device_ids=true, to_apply=%region_20.21 | all-reduce | flops 1 | bytes 8 | tf_op jit(solution)/shard_map/psum | solution.py:194
  2013.0 11.3 multiply_subtract_fusion
  2048.5 6.1 multiply_subtract_fusion.1
  (133 shorter events, 130.5 us)
Async XLA Ops:
  7.2 26.2 %copy-start.2 = (bf16[256,2048]{1,0:T(8,128)(2,1)S(1)}, bf16[256,2048]{1,0:T(8,128)(2,1)}, u32[]{:S(2)}) copy-start(bf16[256,2048]{1,0:T(8,128)(2,1)} %param.18) | copy-start | bytes 3145732
  7.2 26.5 %copy-start.21 = (s32[1,256]{1,0:T(1,128)S(1)}, s32[1,256]{1,0:T(1,128)}, u32[]{:S(2)}) copy-start(s32[1,256]{1,0:T(1,128)} %param.19) | copy-start | bytes 3076
  7.2 105.0 %all-gather.5.cloned.1.call-start = ((), (), s32[]{:S(2)}) async-start(), calls=%async_computation.5 | async-start | bytes 7077888 | tf_op jit(solution)/shard_map/all_gather | solution.py:81
  9.8 152.5 %all-gather.7.cloned.1.call-start = ((), (), s32[]{:S(2)}) async-start(), calls=%async_computation.6 | async-start | bytes 2359296 | tf_op jit(solution)/shard_map/all_gather | solution.py:82
  10.6 205.4 %all-reduce.5.cloned.1.call-start = ((), (), s32[]{:S(2)}) async-start(), calls=%async_computation.7 | async-start | bytes 4194304 | tf_op jit(solution)/shard_map/psum | solution.py:112
  165.9 280.1 %all-gather.9.cloned.1.call-start = ((), (), s32[]{:S(2)}) async-start(), calls=%async_computation.8 | async-start | bytes 18874368 | tf_op jit(solution)/shard_map/all_gather | solution.py:83
  169.8 401.4 %all-gather.11.cloned.1.call-start = ((), (), s32[]{:S(2)}) async-start(), calls=%async_computation.9 | async-start | bytes 9437184 | tf_op jit(solution)/shard_map/all_gather | solution.py:84
  172.6 470.3 %all-reduce.9.cloned.1.call-start = ((), (), s32[]{:S(2)}) async-start(), calls=%async_computation.11 | async-start | bytes 4194304 | tf_op jit(solution)/shard_map/psum | solution.py:131
  593.2 89.0 %all-reduce.7.cloned.1.call-start = ((), (), s32[]{:S(2)}) async-start(), calls=%async_computation.10 | async-start | bytes 2097152 | tf_op jit(solution)/shard_map/psum | solution.py:120
  600.3 159.8 %all-reduce.11.cloned.1.call-start = ((), (), s32[]{:S(2)}) async-start(), calls=%async_computation.12 | async-start | bytes 4194304 | tf_op jit(solution)/shard_map/psum | solution.py:174
  682.2 5.3 copy-start.5
  690.8 4.7 copy-start.19
  708.1 120.3 %reduce-scatter.16.cloned.1.call-start = ((), (), s32[]{:S(2)}) async-start(), calls=%async_computation.17 | async-start | bytes 1179648
  763.8 156.0 %reduce-scatter.10.cloned.1.call-start = ((), (), s32[]{:S(2)}) async-start(), calls=%async_computation.14 | async-start | bytes 4718592 | tf_op jit(solution)/shard_map/reduce_scatter | solution.py:182
  768.2 362.8 %reduce-scatter.8.cloned.1.call-start = ((), (), s32[]{:S(2)}) async-start(), calls=%async_computation.13 | async-start | bytes 14155776 | tf_op jit(solution)/shard_map/reduce_scatter | solution.py:181
  776.6 637.3 %reduce-scatter.14.cloned.1.call-start = ((), (), s32[]{:S(2)}) async-start(), calls=%async_computation.16 | async-start | bytes 18874368 | tf_op jit(solution)/shard_map/reduce_scatter | solution.py:184
  786.3 1169.1 %reduce-scatter.12.cloned.1.call-start = ((), (), s32[]{:S(2)}) async-start(), calls=%async_computation.15 | async-start | bytes 37748736 | tf_op jit(solution)/shard_map/reduce_scatter | solution.py:183
  804.6 5.5 copy-start.14
  1416.7 543.9 %copy-start.1 = (f32[256,2048]{1,0:T(8,128)S(1)}, f32[256,2048]{1,0:T(8,128)}, u32[]{:S(2)}) copy-start(f32[256,2048]{1,0:T(8,128)} %copy-done) | copy-start | bytes 6291460
  2039.7 5.5 copy-start.22
  2039.7 5.5 copy-start.23
  2039.7 6.1 copy-start.12
  2039.7 6.1 copy-start.13
  2039.7 8.8 copy-start.8
  (13 other events, 24.0 us)
Sparse Core Ops, SparseCore 0:
  10.8 101.4 all-gather.4
  115.0 47.2 all-gather.6
  166.1 49.9 all-reduce.4
  218.6 227.3 all-gather.8
  448.5 122.6 all-gather.10
  593.3 49.5 all-reduce.8
  645.8 36.3 all-reduce.6
  708.2 51.8 all-reduce.10
  764.1 64.2 reduce-scatter.15
  832.4 87.3 reduce-scatter.9
  923.4 207.4 reduce-scatter.7
  1134.6 279.2 reduce-scatter.13
  1417.7 537.6 reduce-scatter.11
where the time goes:
time: 2070 us; the launch traced here: 2060 us
  waiting for transfers between devices  1760 us (85%)
  matrix products  98 us (5%)
  local copies, waits for them, and re-layouts  62.6 us (3%)
  blocking collectives  62.2 us (3%)
  other arithmetic  60.2 us (3%)
    reduce_scatter x1, waiting for transfers between devices, on_device(): lax.psum_scatter(grad_lift, 'dp', scatter_dimension=1, tiled=True)  539 us
    reduce_scatter x1, waiting for transfers between devices, on_device(): lax.psum_scatter(grad_down, 'dp', scatter_dimension=0, tiled=True)  279 us
    all_gather x1, waiting for transfers between devices, on_device(): lax.all_gather(lift_weight.astype(bf16), 'dp', axis=1, tiled=True)  228 us
    reduce_scatter x1, waiting for transfers between devices, on_device(): lax.psum_scatter(grad_qkv, 'dp', scatter_dimension=1, tiled=True)  209 us
    all_gather x1, waiting for transfers between devices, on_device(): lax.all_gather(down_weight.astype(bf16), 'dp', axis=0, tiled=True)  115 us
    reduce_scatter x1, waiting for transfers between devices, on_device(): lax.psum_scatter(grad_out, 'dp', scatter_dimension=0, tiled=True)  89.2 us
    all_gather x1, waiting for transfers between devices, on_device(): lax.all_gather(qkv_weight.astype(bf16), 'dp', axis=1, tiled=True)  78.4 us
    unnamed x62, local copies, waits for them, and re-layouts  55 us
  transfers between devices with their start and end apart: 13, of which 13 were waited for; matrix products, arithmetic and copies ran while one was open for 5% of the time, Pallas kernels for 0%

commit v1 on v0

--- a/solution.py
+++ b/solution.py
@@ -231,6 +231,296 @@
     )
 
 
+def swap_core(v):
+    return lax.ppermute(v, "tensor", [(i, i ^ 1) for i in range(lax.axis_size("tensor"))])
+
+
+def swap_x(v):
+    return lax.ppermute(v, "tensor", [(i, i ^ 2) for i in range(lax.axis_size("tensor"))])
+
+
+def swap_dp(v, mask):
+    return lax.ppermute(v, "dp", [(i, i ^ mask) for i in range(lax.axis_size("dp"))])
+
+
+def shift_z(v, step):
+    size = lax.axis_size("dp")
+    return lax.ppermute(v, "dp", [(i, (i + 2 * step) % size) for i in range(size)])
+
+
+def in_order(first, mine, other, axis):
+    return jnp.where(
+        first,
+        jnp.concatenate([mine, other], axis),
+        jnp.concatenate([other, mine], axis),
+    )
+
+
+def gather_rows(own):
+    ring = [own]
+    for _ in range(lax.axis_size("dp") // 2 - 1):
+        ring.append(shift_z(ring[-1], 1))
+    return jnp.concatenate(ring + [swap_dp(piece, 1) for piece in ring], 0)
+
+
+def scatter_rows(partial, rows):
+    f32 = jnp.float32
+    bf16 = jnp.bfloat16
+    ring = lax.axis_size("dp") // 2
+    slots = partial.reshape(2, ring, rows, partial.shape[-1])
+    held = None
+    for step in range(ring - 1, -1, -1):
+        here = slots[0, step] + swap_dp(slots[1, step].astype(bf16), 1).astype(f32)
+        held = here if held is None else here + shift_z(held.astype(bf16), -1).astype(f32)
+    held = held.astype(bf16)
+    return held.astype(f32) + swap_x(held).astype(f32)
+
+
+def on_device_wide(
+    tokens,
+    documents,
+    cotangent,
+    qkv_weight,
+    out_weight,
+    lift_weight,
+    down_weight,
+    gains,
+    qkv_first,
+    out_first,
+    lift_first,
+    down_first,
+    gains_first,
+    qkv_second,
+    out_second,
+    lift_second,
+    down_second,
+    gains_second,
+):
+    bf16 = jnp.bfloat16
+    f32 = jnp.float32
+    size = lax.axis_size("dp")
+    ring = size // 2
+    place = lax.axis_index("dp")
+    core = lax.axis_index("tensor") % 2
+    first = core == 0
+    length, width = tokens.shape
+    half = length // 2
+    block = qkv_weight.shape[1]
+    units = lift_weight.shape[2] // size
+    scale = 1.0 / math.sqrt(HD)
+    offset = -math.log(length)
+
+    def own_half(v):
+        return lax.dynamic_slice_in_dim(v, core * half, half, 0)
+
+    def dot(a, b):
+        return jnp.dot(a, b, preferred_element_type=f32)
+
+    def dot_t(a, b):
+        return lax.dot_general(a, b, (((1,), (1,)), ((), ())), preferred_element_type=f32)
+
+    def t_dot(a, b):
+        return lax.dot_general(a, b, (((0,), (0,)), ((), ())), preferred_element_type=f32)
+
+    w_gains = lax.all_gather(gains.astype(bf16), "dp", axis=1, tiled=True)
+    all_docs = lax.all_gather(documents, "dp", axis=0, tiled=True)
+    gain_one = w_gains[0].astype(f32)
+    gain_two = w_gains[1].astype(f32)
+
+    x_rows = own_half(tokens).astype(f32)
+    own_cot = own_half(cotangent)
+    scaled_one, inverse_one, normed_one = norm_forward(x_rows, gain_one)
+    normed_one = gather_rows(normed_one)
+
+    qkv_low = qkv_weight.astype(bf16).reshape(3, 2, block // 2, qkv_weight.shape[2])
+    keep = lax.dynamic_index_in_dim(qkv_low, core, 1, keepdims=False)
+    give = lax.dynamic_index_in_dim(qkv_low, 1 - core, 1, keepdims=False)
+    plane = in_order(first, keep, swap_core(give), 2)
+    w_head = jnp.zeros((size, block // 2, 3 * HD), bf16)
+    for delta in range(size):
+        piece = lax.dynamic_slice_in_dim(plane, (place ^ delta) * HD, HD, 2)
+        piece = jnp.concatenate([piece[0], piece[1], piece[2]], 1)
+        if delta:
+            piece = swap_dp(piece, delta)
+        w_head = lax.dynamic_update_slice_in_dim(w_head, piece[None], place ^ delta, 0)
+    w_head = w_head.reshape(size, 1, block // 2, 3 * HD)
+    w_head = in_order(first, w_head, swap_core(w_head), 1).reshape(width, 3 * HD)
+
+    to_head = [
+        (4 * d + 2 * x + c, 4 * ((size // 2) * c + d // 2) + 2 * x + d % 2)
+        for d in range(size)
+        for x in range(2)
+        for c in range(2)
+    ]
+    w_rows = lax.ppermute(out_weight.astype(bf16), ("dp", "tensor"), to_head)
+    w_rows = in_order(first, w_rows, swap_core(w_rows), 0)
+
+    lift_mine = jnp.zeros((width, 2 * units), bf16)
+    for delta in range(size):
+        piece = lax.dynamic_slice_in_dim(lift_weight, (place ^ delta) * units, units, 2)
+        piece = jnp.concatenate([piece[0], piece[1]], 1).astype(bf16)
+        if delta:
+            piece = swap_dp(piece, delta)
+        lift_mine = lax.dynamic_update_slice_in_dim(lift_mine, piece, (place ^ delta) * block, 0)
+    lift_other = swap_core(lift_mine)
+    w_lift = jnp.concatenate(
+        [lift_mine[:, :units], lift_other[:, :units], lift_mine[:, units:], lift_other[:, units:]], 1
+    )
+    down_mine = down_weight.astype(bf16)
+    w_down = jnp.concatenate([down_mine, swap_core(down_mine)], 0)
+    all_cot = gather_rows(own_cot)
+
+    def to_sequences(v):
+        v = v.reshape(2, ring, half, v.shape[-1])
+        keep = lax.dynamic_index_in_dim(v, core, 0, keepdims=False)
+        give = lax.dynamic_index_in_dim(v, 1 - core, 0, keepdims=False)
+        return in_order(first, keep, swap_core(give), 1)
+
+    def to_halves(v):
+        v = v.reshape(ring, 2, half, v.shape[-1])
+        keep = lax.dynamic_index_in_dim(v, core, 1, keepdims=False)
+        give = lax.dynamic_index_in_dim(v, 1 - core, 1, keepdims=False)
+        joined = in_order(first, keep[None], swap_core(give)[None], 0)
+        return joined.reshape(2 * ring * half, v.shape[-1])
+
+    project = to_sequences(dot(normed_one, w_head).astype(bf16))
+    queries = project[:, :, :HD]
+    keys = project[:, :, HD : 2 * HD]
+    values = project[:, :, 2 * HD :]
+    owners = ((place // 2 - jnp.arange(ring, dtype=jnp.int32)) % ring) * 2 + (place % 2 ^ core)
+    docs = all_docs[owners]
+    pos = jnp.arange(length, dtype=jnp.int32)
+    allowed = (pos[:, None] >= pos[None, :])[None] & (docs[:, :, None] == docs[:, None, :])
+    scores = jnp.einsum("sqd,skd->sqk", queries, keys, preferred_element_type=f32) * scale + offset
+    probs = jnp.where(allowed, jax.nn.sigmoid(scores), 0.0)
+    probs_low = probs.astype(bf16)
+    attended = jnp.einsum("sqk,skd->sqd", probs_low, values, preferred_element_type=f32)
+    attended = to_halves(attended.astype(bf16))
+    middle = x_rows + scatter_rows(dot(attended, w_rows), half)
+    scaled_two, inverse_two, normed_two = norm_forward(middle, gain_two)
+    normed_two = gather_rows(normed_two)
+
+    gate_up = dot(normed_two, w_lift)
+    gate = gate_up[:, : 2 * units]
+    upward = gate_up[:, 2 * units :]
+    sigma = jax.nn.sigmoid(gate)
+    hidden = (gate * sigma * upward).astype(bf16)
+    grad_hidden = dot_t(all_cot, w_down)
+    grad_gate = (grad_hidden * upward * sigma * (1.0 + gate * (1.0 - sigma))).astype(bf16)
+    grad_up = (grad_hidden * gate * sigma).astype(bf16)
+    grad_pair = jnp.concatenate([grad_gate, grad_up], 1)
+    back_two = scatter_rows(dot_t(grad_pair, w_lift), half)
+    grad_gain_two, grad_mid_norm = norm_backward(back_two, scaled_two, inverse_two, gain_two)
+    grad_mid = own_cot.astype(f32) + grad_mid_norm
+    all_branch = gather_rows(grad_mid.astype(bf16))
+
+    feed = scatter_rows(dot(hidden, w_down), half)
+    layer_half = (middle + feed).astype(bf16)
+    layer_out = in_order(first, layer_half, swap_core(layer_half), 0)
+
+    grad_down = t_dot(hidden, all_cot)
+    red_down = grad_down[:block] + swap_core(grad_down[block:])
+    lift_give = t_dot(
+        normed_two, jnp.concatenate([grad_gate[:, units:], grad_up[:, units:]], 1)
+    )
+    lift_keep = t_dot(
+        normed_two, jnp.concatenate([grad_gate[:, :units], grad_up[:, :units]], 1)
+    )
+    lift_sum = (lift_keep + swap_core(lift_give)).astype(bf16)
+    red_lift = jnp.zeros(lift_weight.shape, f32)
+    for delta in range(size):
+        piece = lax.dynamic_slice_in_dim(lift_sum, (place ^ delta) * block, block, 0)
+        if delta:
+            piece = swap_dp(piece, delta)
+        piece = jnp.stack([piece[:, :units], piece[:, units:]]).astype(f32)
+        red_lift = lax.dynamic_update_slice_in_dim(red_lift, piece, (place ^ delta) * units, 2)
+
+    grad_out = t_dot(attended, all_branch)
+    rows = HD // 2
+    out_keep = lax.dynamic_slice_in_dim(grad_out, core * rows, rows, 0)
+    out_give = lax.dynamic_slice_in_dim(grad_out, (1 - core) * rows, rows, 0)
+    red_out = (out_keep + swap_core(out_give)).astype(bf16)
+    red_out = lax.ppermute(red_out, ("dp", "tensor"), [(b, a) for a, b in to_head]).astype(f32)
+
+    grad_heads = to_sequences(dot_t(all_branch, w_rows).astype(bf16))
+    grad_probs = jnp.einsum("sqd,skd->sqk", grad_heads, values, preferred_element_type=f32)
+    grad_scores = (grad_probs * probs * (1.0 - probs)).astype(bf16)
+    grad_queries = jnp.einsum("sqk,skd->sqd", grad_scores, keys, preferred_element_type=f32) * scale
+    grad_keys = jnp.einsum("sqk,sqd->skd", grad_scores, queries, preferred_element_type=f32) * scale
+    grad_values = jnp.einsum("sqk,sqd->skd", probs_low, grad_heads, preferred_element_type=f32)
+    grad_project = to_halves(
+        jnp.concatenate([grad_queries, grad_keys, grad_values], 2).astype(bf16)
+    )
+    back_one = scatter_rows(dot_t(grad_project, w_head), half)
+
+    grad_head = t_dot(normed_one, grad_project).reshape(size, 2, block // 2, 3 * HD)
+    keep = lax.dynamic_index_in_dim(grad_head, core, 1, keepdims=False)
+    give = lax.dynamic_index_in_dim(grad_head, 1 - core, 1, keepdims=False)
+    grad_head = (keep + swap_core(give)).astype(bf16)
+    by_head = jnp.zeros(grad_head.shape, bf16)
+    for delta in range(size):
+        piece = lax.dynamic_slice_in_dim(grad_head, place ^ delta, 1, 0)
+        if delta:
+            piece = swap_dp(piece, delta)
+        by_head = lax.dynamic_update_slice_in_dim(by_head, piece, place ^ delta, 0)
+    keep = lax.dynamic_slice_in_dim(by_head, core * ring, ring, 0)
+    give = lax.dynamic_slice_in_dim(by_head, (1 - core) * ring, ring, 0)
+    red_qkv = in_order(first, keep, swap_core(give), 1)
+    red_qkv = red_qkv.reshape(ring, block, 3, HD).transpose(2, 1, 0, 3)
+    red_qkv = red_qkv.reshape(qkv_weight.shape).astype(f32)
+
+    grad_gain_one, grad_x_norm = norm_backward(back_one, scaled_one, inverse_one, gain_one)
+    tokens_half = grad_mid + grad_x_norm
+    grad_tokens = in_order(first, tokens_half, swap_core(tokens_half), 0)
+
+    grad_gains = 0.5 * jnp.stack([grad_gain_one, grad_gain_two])
+    local_total = (
+        jnp.sum(red_qkv * red_qkv)
+        + jnp.sum(red_out * red_out)
+        + jnp.sum(red_lift * red_lift)
+        + jnp.sum(red_down * red_down)
+    )
+    grad_gains, total = lax.psum((grad_gains, local_total), ("dp", "tensor"))
+    grad_norm = jnp.sqrt(total + jnp.sum(grad_gains * grad_gains))
+    red_gains = lax.dynamic_slice_in_dim(grad_gains, place * gains.shape[1], gains.shape[1], 1)
+    factor = CLIP_NORM / jnp.maximum(grad_norm, CLIP_NORM)
+    qkv_new, qkv_moment, qkv_variance = adam_step(
+        qkv_weight, qkv_first, qkv_second, red_qkv, factor, rate_matrix, decay_matrix
+    )
+    out_new, out_moment, out_variance = adam_step(
+        out_weight, out_first, out_second, red_out, factor, rate_matrix, decay_matrix
+    )
+    lift_new, lift_moment, lift_variance = adam_step(
+        lift_weight, lift_first, lift_second, red_lift, factor, rate_matrix, decay_matrix
+    )
+    down_new, down_moment, down_variance = adam_step(
+        down_weight, down_first, down_second, red_down, factor, rate_matrix, decay_matrix
+    )
+    gains_new, gains_moment, gains_variance = adam_step(
+        gains, gains_first, gains_second, red_gains, factor, rate_gain, 0.0
+    )
+    return (
+        layer_out,
+        grad_tokens,
+        qkv_new,
+        out_new,
+        lift_new,
+        down_new,
+        gains_new,
+        qkv_moment,
+        out_moment,
+        lift_moment,
+        down_moment,
+        gains_moment,
+        qkv_variance,
+        out_variance,
+        lift_variance,
+        down_variance,
+        gains_variance,
+        grad_norm,
+    )
+
+
 def solution(mesh):
     placed = (
         P("dp", None),
@@ -252,8 +542,13 @@
         P(("tensor", "dp"), None),
         P(None, "dp"),
     )
+    def layer(*arrays):
+        plane_heads = 2 * arrays[3].shape[2] // HD
+        wide = lax.axis_size("tensor") == 4 and lax.axis_size("dp") == plane_heads
+        return (on_device_wide if wide else on_device)(*arrays)
+
     return jax.shard_map(
-        on_device,
+        layer,
         mesh=mesh,
         in_specs=placed,
         out_specs=(

time: 2070 us -> 805 us (0.39)
  waiting for transfers between devices: 1760 us -> 306 us
  starting transfers between devices: 1.45 us -> 206 us
  matrix products: 98 us -> 46.3 us
  blocking collectives: 62.2 us -> 89 us
    reduce_scatter x4 -> x0, waiting for transfers between devices: 1120 us -> none  [the longest x1 539 us: on_device(): lax.psum_scatter(grad_lift, 'dp', scatter_dimension=1, tiled=True)]
    all_gather x4 -> x0, waiting for transfers between devices: 464 us -> none  [the longest x1 228 us: on_device(): lax.all_gather(lift_weight.astype(bf16), 'dp', axis=1, tiled=True)]
    ppermute x0 -> x106, waiting for transfers between devices: none -> 306 us  [the longest x60 198 us: swap_dp(): lax.ppermute(v, 'dp', [(i, i ^ mask) for i in range(lax.axis_size('dp'))])]
    ppermute x0 -> x106, starting transfers between devices: none -> 206 us  [the longest x24 107 us: shift_z(): lax.ppermute(v, 'dp', [(i, (i + 2 * step) % size) for i in range(size)])]
    psum x4 -> x0, waiting for transfers between devices: 174 us -> none  [the longest x1 52 us: on_device(): lax.psum(jnp.einsum('cte,cde->td', grad_project, w_qkv, preferred_element...]
    dot_general x18 -> x19, matrix products: 98 us -> 46.3 us  [the longest x4 15.9 us: dot_t(): lax.dot_general(a, b, (((1,), (1,)), ((), ())), preferred_element_type=f32)]
    unnamed x62 -> x158, local copies, waits for them, and re-layouts: 55 us -> 25.8 us
    all_gather x1 -> x2, blocking collectives: 22.7 us -> 47 us  [the longest x1 25.2 us: on_device_wide(): all_docs = lax.all_gather(documents, 'dp', axis=0, tiled=True)]
  transfers between devices with their start and end apart: 13 -> 106, of which waited for: 13 -> 53; matrix products, arithmetic and copies ran while one was open for 5% -> 19% of each run, Pallas kernels for 0% -> 0%
where the time goes in v1:
time: 805 us; the launch traced here: 795 us
  waiting for transfers between devices  306 us (38%)
  starting transfers between devices  206 us (26%)
  blocking collectives  89 us (11%)
  other arithmetic  75.4 us (9%)
  local copies, waits for them, and re-layouts  64.4 us (8%)
  matrix products  46.3 us (6%)
    ppermute x60, waiting for transfers between devices, swap_dp(): lax.ppermute(v, 'dp', [(i, i ^ mask) for i in range(lax.axis_size('dp'))])  198 us
    ppermute x24, starting transfers between devices, shift_z(): lax.ppermute(v, 'dp', [(i, (i + 2 * step) % size) for i in range(size)])  107 us
    ppermute x24, waiting for transfers between devices, shift_z(): lax.ppermute(v, 'dp', [(i, (i + 2 * step) % size) for i in range(size)])  100 us
    ppermute x60, starting transfers between devices, swap_dp(): lax.ppermute(v, 'dp', [(i, i ^ mask) for i in range(lax.axis_size('dp'))])  84.6 us
    psum x1, blocking collectives, on_device_wide(): grad_gains, total = lax.psum((grad_gains, local_total), ('dp', 'tensor'))  41.9 us
    unnamed x158, local copies, waits for them, and re-layouts  25.8 us
    all_gather x1, blocking collectives, on_device_wide(): all_docs = lax.all_gather(documents, 'dp', axis=0, tiled=True)  25.2 us
    all_gather x1, blocking collectives, on_device_wide(): w_gains = lax.all_gather(gains.astype(bf16), 'dp', axis=1, tiled=True)  21.8 us
  transfers between devices with their start and end apart: 106, of which 53 were waited for; matrix products, arithmetic and copies ran while one was open for 19% of the time, Pallas kernels for 0%

profile of v1, /device:TPU:0, one launch (start us, length us, event | category | flops | bytes accessed | tf_op | source)
XLA Modules:
  0.0 795.5 jit_solution(6171949235313984629)
XLA Ops:
  4.3 21.8 %all_gather.7 = bf16[2,2048]{1,0:T(2,128)(2,1)S(1)} all-gather(bf16[2,256]{1,0:T(2,128)(2,1)S(1)} %convert_element_type.332), channel_id=1, replica_groups=mesh['dp'=8,'tensor'=4] {'dp'}, dimensions={1}, use_global_device_ids=true | all-gather | bytes 9216 | tf_op jit(solution)/shard_map/all_gather | solution.py:325
  34.8 9.5 %collective-permute-done.8 = bf16[128,384]{1,0:T(8,128)(2,1)S(1)} collective-permute-done((bf16[128,384]{1,0:T(8,128)(2,1)S(1)}, bf16[128,384]{1,0:T(8,128)(2,1)S(1)}, u32[]{:S(2)}, u32[]{:S(2)}) %collective-permute-start.8) | collective-permute-done | bytes 98336 | tf_op jit(solution)/shard_map/ppermute | solution.py:243
  75.3 15.3 %collective-permute-start.2 = (bf16[128,2048]{1,0:T(8,128)(2,1)S(1)}, bf16[128,2048]{1,0:T(8,128)(2,1)S(1)}, u32[]{:S(2)}, u32[]{:S(2)}) collective-permute-start(bf16[128,2048]{1,0:T(8,128)(2,1)S(1)} %collective-permute-done.1), channel_id=1, source_target_pairs={{0,8},{4,12},{8,16},{12,20},{16,24},{20,28},{24,0},{28,4},{1,9},{5... | collective-permute-start | bytes 1572872 | tf_op jit(solution)/shard_map/ppermute | solution.py:248
  91.1 11.1 %collective-permute-done.2 = bf16[128,2048]{1,0:T(8,128)(2,1)S(1)} collective-permute-done((bf16[128,2048]{1,0:T(8,128)(2,1)S(1)}, bf16[128,2048]{1,0:T(8,128)(2,1)S(1)}, u32[]{:S(2)}, u32[]{:S(2)}) %collective-permute-start.2) | collective-permute-done | bytes 524320 | tf_op jit(solution)/shard_map/ppermute | solution.py:248
  105.0 10.7 %collective-permute-done.6 = bf16[128,2048]{1,0:T(8,128)(2,1)S(1)} collective-permute-done((bf16[128,2048]{1,0:T(8,128)(2,1)S(1)}, bf16[128,2048]{1,0:T(8,128)(2,1)S(1)}, u32[]{:S(2)}, u32[]{:S(2)}) %collective-permute-start.6) | collective-permute-done | bytes 524320 | tf_op jit(solution)/shard_map/ppermute | solution.py:243
  119.4 25.2 %all-gather = s32[8,1,256]{2,1,0:T(1,128)S(1)} all-gather(s32[1,1,256]{2,1,0:T(1,128)S(1)} %bitcast.418), channel_id=1, replica_groups=mesh['dp'=8,'tensor'=4] {'dp'}, dimensions={0}, use_global_device_ids=true | all-gather | bytes 9216 | tf_op jit(solution)/shard_map/all_gather | solution.py:326
  156.0 15.1 %collective-permute-done.23 = bf16[128,2048]{1,0:T(8,128)(2,1)S(1)} collective-permute-done((bf16[128,2048]{1,0:T(8,128)(2,1)S(1)}, bf16[128,2048]{1,0:T(8,128)(2,1)S(1)}, u32[]{:S(2)}, u32[]{:S(2)}) %collective-permute-start.23) | collective-permute-done | bytes 524320 | tf_op jit(solution)/shard_map/ppermute | solution.py:243
  202.0 27.9 %collective-permute-start.53 = (bf16[128,2048]{1,0:T(8,128)(2,1)S(1)}, bf16[128,2048]{1,0:T(8,128)(2,1)S(1)}, u32[]{:S(2)}, u32[]{:S(2)}) collective-permute-start(bf16[128,2048]{1,0:T(8,128)(2,1)S(1)} %get-tuple-element.78), channel_id=1, source_target_pairs={{0,8},{4,12},{8,16},{12,20},{16,24},{20,28},{24,0},{28,4},{1,9},{5... | collective-permute-start | bytes 1572872 | tf_op jit(solution)/shard_map/ppermute | solution.py:248
  242.9 8.9 %collective-permute-done.41 = bf16[256,512]{1,0:T(8,128)(2,1)S(1)} collective-permute-done((bf16[256,512]{1,0:T(8,128)(2,1)S(1)}, bf16[256,512]{1,0:T(8,128)(2,1)S(1)}, u32[]{:S(2)}, u32[]{:S(2)}) %collective-permute-start.41) | collective-permute-done | bytes 262176 | tf_op jit(solution)/shard_map/ppermute | solution.py:243
  251.9 26.6 %collective-permute-start.54 = (bf16[128,2048]{1,0:T(8,128)(2,1)S(1)}, bf16[128,2048]{1,0:T(8,128)(2,1)S(1)}, u32[]{:S(2)}, u32[]{:S(2)}) collective-permute-start(bf16[128,2048]{1,0:T(8,128)(2,1)S(1)} %collective-permute-done.53), channel_id=1, source_target_pairs={{0,8},{4,12},{8,16},{12,20},{16,24},{20,28},{24,0},{28,4},{1,9},{5... | collective-permute-start | bytes 1572872 | tf_op jit(solution)/shard_map/ppermute | solution.py:248
  281.7 8.6 %collective-permute-done.54 = bf16[128,2048]{1,0:T(8,128)(2,1)S(1)} collective-permute-done((bf16[128,2048]{1,0:T(8,128)(2,1)S(1)}, bf16[128,2048]{1,0:T(8,128)(2,1)S(1)}, u32[]{:S(2)}, u32[]{:S(2)}) %collective-permute-start.54) | collective-permute-done | bytes 524320 | tf_op jit(solution)/shard_map/ppermute | solution.py:248
  293.7 13.2 %collective-permute-done.55 = bf16[128,2048]{1,0:T(8,128)(2,1)S(1)} collective-permute-done((bf16[128,2048]{1,0:T(8,128)(2,1)S(1)}, bf16[128,2048]{1,0:T(8,128)(2,1)S(1)}, u32[]{:S(2)}, u32[]{:S(2)}) %collective-permute-start.55) | collective-permute-done | bytes 524320 | tf_op jit(solution)/shard_map/ppermute | solution.py:248
  334.5 10.0 %collective-permute-done.30 = bf16[128,2048]{1,0:T(8,128)(2,1)S(1)} collective-permute-done((bf16[128,2048]{1,0:T(8,128)(2,1)S(1)}, bf16[128,2048]{1,0:T(8,128)(2,1)S(1)}, u32[]{:S(2)}, u32[]{:S(2)}) %collective-permute-start.30) | collective-permute-done | bytes 524320 | tf_op jit(solution)/shard_map/ppermute | solution.py:248
  346.1 11.2 %collective-permute-done.32 = bf16[128,2048]{1,0:T(8,128)(2,1)S(1)} collective-permute-done((bf16[128,2048]{1,0:T(8,128)(2,1)S(1)}, bf16[128,2048]{1,0:T(8,128)(2,1)S(1)}, u32[]{:S(2)}, u32[]{:S(2)}) %collective-permute-start.32) | collective-permute-done | bytes 524320 | tf_op jit(solution)/shard_map/ppermute | solution.py:243
  357.3 11.2 %collective-permute-done.33 = bf16[128,2048]{1,0:T(8,128)(2,1)S(1)} collective-permute-done((bf16[128,2048]{1,0:T(8,128)(2,1)S(1)}, bf16[128,2048]{1,0:T(8,128)(2,1)S(1)}, u32[]{:S(2)}, u32[]{:S(2)}) %collective-permute-start.33) | collective-permute-done | bytes 524320 | tf_op jit(solution)/shard_map/ppermute | solution.py:243
  400.2 10.7 %collective-permute-done.63 = bf16[128,2048]{1,0:T(8,128)(2,1)S(1)} collective-permute-done((bf16[128,2048]{1,0:T(8,128)(2,1)S(1)}, bf16[128,2048]{1,0:T(8,128)(2,1)S(1)}, u32[]{:S(2)}, u32[]{:S(2)}) %collective-permute-start.63) | collective-permute-done | bytes 524320 | tf_op jit(solution)/shard_map/ppermute | solution.py:243
  433.6 9.7 %collective-permute-done.65 = bf16[128,2048]{1,0:T(8,128)(2,1)S(1)} collective-permute-done((bf16[128,2048]{1,0:T(8,128)(2,1)S(1)}, bf16[128,2048]{1,0:T(8,128)(2,1)S(1)}, u32[]{:S(2)}, u32[]{:S(2)}) %collective-permute-start.65) | collective-permute-done | bytes 524320 | tf_op jit(solution)/shard_map/ppermute | solution.py:248
  514.9 8.7 %collective-permute-done.69 = bf16[128,2048]{1,0:T(8,128)(2,1)S(1)} collective-permute-done((bf16[128,2048]{1,0:T(8,128)(2,1)}, bf16[128,2048]{1,0:T(8,128)(2,1)S(1)}, u32[]{:S(2)}, u32[]{:S(2)}) %collective-permute-start.69) | collective-permute-done | bytes 524320 | tf_op jit(solution)/shard_map/ppermute | solution.py:248
  541.7 13.5 %collective-permute-done.73 = bf16[128,2048]{1,0:T(8,128)(2,1)S(1)} collective-permute-done((bf16[128,2048]{1,0:T(8,128)(2,1)S(1)}, bf16[128,2048]{1,0:T(8,128)(2,1)S(1)}, u32[]{:S(2)}, u32[]{:S(2)}) %collective-permute-start.73) | collective-permute-done | bytes 524320 | tf_op jit(solution)/shard_map/ppermute | solution.py:243
  566.7 13.4 %collective-permute-done.102 = bf16[256,512]{1,0:T(8,128)(2,1)S(1)} collective-permute-done((bf16[256,512]{1,0:T(8,128)(2,1)S(1)}, bf16[256,512]{1,0:T(8,128)(2,1)S(1)}, u32[]{:S(2)}, u32[]{:S(2)}) %collective-permute-start.102) | collective-permute-done | bytes 262176 | tf_op jit(solution)/shard_map/ppermute | solution.py:243
  661.6 9.6 %collective-permute-done.92 = bf16[1,128,384]{2,1,0:T(8,128)(2,1)} collective-permute-done((bf16[1,128,384]{2,1,0:T(8,128)(2,1)}, bf16[1,128,384]{2,1,0:T(8,128)(2,1)}, u32[]{:S(2)}, u32[]{:S(2)}) %collective-permute-start.92) | collective-permute-done | bytes 98336 | tf_op jit(solution)/shard_map/ppermute | solution.py:243
  671.2 10.5 %collective-permute-start.93 = (bf16[1,128,384]{2,1,0:T(8,128)(2,1)}, bf16[1,128,384]{2,1,0:T(8,128)(2,1)}, u32[]{:S(2)}, u32[]{:S(2)}) collective-permute-start(bf16[1,128,384]{2,1,0:T(8,128)(2,1)} %get-tuple-element.133), channel_id=1, source_target_pairs={{0,28},{4,24},{8,20},{12,16},{16,12},{20,8},{24,4},{28,0},{1,29},{... | collective-permute-start | bytes 294920 | tf_op jit(solution)/shard_map/ppermute | solution.py:243
  711.5 41.9 %all-reduce = (f32[]{:T(128)}, f32[2,2048]{1,0:T(2,128)S(1)}) all-reduce(f32[]{:T(128)S(6)} %add.524, f32[2,2048]{1,0:T(2,128)S(1)} %maximum_multiply_fusion), channel_id=1, replica_groups=mesh['dp'=8,'tensor'=4] {'dp','tensor'}, use_global_device_ids=true, to_apply=%region_8.9 | all-reduce | flops 4097 | bytes 32776 | tf_op jit(solution)/shard_map/psum | solution.py:483
  757.9 10.0 %multiply_subtract_fusion = (f32[2,256,2048]{2,1,0:T(8,128)}, f32[2,256,2048]{2,1,0:T(8,128)}, f32[2,256,2048]{2,1,0:T(8,128)}) fusion(f32[2,256,2048]{2,1,0:T(8,128)} %param.23, f32[2,256,2048]{2,1,0:T(8,128)S(1)} %copy-done.2, f32[]{:T(128)S(6)} %div.113, f32[2,256,2048]{2,1,0:T(8,128)} %param.28, f32[2,256,2048]{2,1,0:T(8,128)} %param.33), kind=kLoop, calls=%fused_computation.4 | loop fusion | flops 16777216 | bytes 29360132 | tf_op jit(solution)/shard_map/sub | solution.py:55
  (526 shorter events, 433.3 us)
Async XLA Ops:
  27.6 74.9 %collective-permute-start.3 = (bf16[128,2048]{1,0:T(8,128)(2,1)}, bf16[128,2048]{1,0:T(8,128)(2,1)}, u32[]{:S(2)}, u32[]{:S(2)}) collective-permute-start(bf16[128,2048]{1,0:T(8,128)(2,1)} %get-tuple-element.84), channel_id=1, source_target_pairs={{0,4},{4,0},{8,12},{12,8},{16,20},{20,16},{24,28},{28,24},{1,5},{5... | collective-permute-start | bytes 1572872 | tf_op jit(solution)/shard_map/ppermute | solution.py:243
  28.3 117.0 %collective-permute-start.18 = (bf16[64,2048]{1,0:T(8,128)(2,1)}, bf16[64,2048]{1,0:T(8,128)(2,1)}, u32[]{:S(2)}, u32[]{:S(2)}) collective-permute-start(bf16[64,2048]{1,0:T(8,128)(2,1)} %convert_element_type.338), channel_id=1, source_target_pairs={{0,0},{1,16},{2,2},{3,18},{4,1},{5,17},{6,3},{7,19},{8,4},{9,20},{... | collective-permute-start | bytes 786440 | tf_op jit(solution)/shard_map/ppermute | solution.py:355
  119.1 71.0 %collective-permute-start.35 = (bf16[256,512]{1,0:T(8,128)(2,1)}, bf16[256,512]{1,0:T(8,128)(2,1)}, u32[]{:S(2)}, u32[]{:S(2)}) collective-permute-start(bf16[256,512]{1,0:T(8,128)(2,1)} %pad_maximum_fusion.7), channel_id=1, source_target_pairs={{0,4},{4,0},{8,12},{12,8},{16,20},{20,16},{24,28},{28,24},{1,5},{5... | collective-permute-start | bytes 786440 | tf_op jit(solution)/shard_map/ppermute | solution.py:243
  152.2 39.0 %collective-permute-start.36 = (bf16[256,512]{1,0:T(8,128)(2,1)S(1)}, bf16[256,512]{1,0:T(8,128)(2,1)S(1)}, u32[]{:S(2)}, u32[]{:S(2)}) collective-permute-start(bf16[256,512]{1,0:T(8,128)(2,1)S(1)} %pad_maximum_fusion.8), channel_id=1, source_target_pairs={{0,8},{4,12},{8,0},{12,4},{16,24},{20,28},{24,16},{28,20},{1,9},{5... | collective-permute-start | bytes 786440 | tf_op jit(solution)/shard_map/ppermute | solution.py:243
  153.8 76.3 %collective-permute-start.37 = (bf16[256,512]{1,0:T(8,128)(2,1)S(1)}, bf16[256,512]{1,0:T(8,128)(2,1)S(1)}, u32[]{:S(2)}, u32[]{:S(2)}) collective-permute-start(bf16[256,512]{1,0:T(8,128)(2,1)S(1)} %pad_maximum_fusion.9), channel_id=1, source_target_pairs={{0,12},{4,8},{8,4},{12,0},{16,28},{20,24},{24,20},{28,16},{1,13},{... | collective-permute-start | bytes 786440 | tf_op jit(solution)/shard_map/ppermute | solution.py:243
  190.1 44.9 %collective-permute-start.38 = (bf16[256,512]{1,0:T(8,128)(2,1)S(1)}, bf16[256,512]{1,0:T(8,128)(2,1)S(1)}, u32[]{:S(2)}, u32[]{:S(2)}) collective-permute-start(bf16[256,512]{1,0:T(8,128)(2,1)S(1)} %pad_maximum_fusion.10), channel_id=1, source_target_pairs={{0,16},{4,20},{8,24},{12,28},{16,0},{20,4},{24,8},{28,12},{1,17},{... | collective-permute-start | bytes 786440 | tf_op jit(solution)/shard_map/ppermute | solution.py:243
  191.2 49.1 %collective-permute-start.39 = (bf16[256,512]{1,0:T(8,128)(2,1)S(1)}, bf16[256,512]{1,0:T(8,128)(2,1)S(1)}, u32[]{:S(2)}, u32[]{:S(2)}) collective-permute-start(bf16[256,512]{1,0:T(8,128)(2,1)S(1)} %pad_maximum_fusion.11), channel_id=1, source_target_pairs={{0,20},{4,16},{8,28},{12,24},{16,4},{20,0},{24,12},{28,8},{1,21},{... | collective-permute-start | bytes 786440 | tf_op jit(solution)/shard_map/ppermute | solution.py:243
  195.0 45.4 %collective-permute-start.40 = (bf16[256,512]{1,0:T(8,128)(2,1)S(1)}, bf16[256,512]{1,0:T(8,128)(2,1)S(1)}, u32[]{:S(2)}, u32[]{:S(2)}) collective-permute-start(bf16[256,512]{1,0:T(8,128)(2,1)S(1)} %pad_maximum_fusion.12), channel_id=1, source_target_pairs={{0,24},{4,28},{8,16},{12,20},{16,8},{20,12},{24,0},{28,4},{1,25},{... | collective-permute-start | bytes 786440 | tf_op jit(solution)/shard_map/ppermute | solution.py:243
  202.0 49.9 %collective-permute-start.53 = (bf16[128,2048]{1,0:T(8,128)(2,1)S(1)}, bf16[128,2048]{1,0:T(8,128)(2,1)S(1)}, u32[]{:S(2)}, u32[]{:S(2)}) collective-permute-start(bf16[128,2048]{1,0:T(8,128)(2,1)S(1)} %get-tuple-element.78), channel_id=1, source_target_pairs={{0,8},{4,12},{8,16},{12,20},{16,24},{20,28},{24,0},{28,4},{1,9},{5... | collective-permute-start | bytes 1572872 | tf_op jit(solution)/shard_map/ppermute | solution.py:248
  230.1 48.4 %collective-permute-start.20 = (bf16[128,2048]{1,0:T(8,128)(2,1)S(1)}, bf16[128,2048]{1,0:T(8,128)(2,1)S(1)}, u32[]{:S(2)}, u32[]{:S(2)}) collective-permute-start(bf16[128,2048]{1,0:T(8,128)(2,1)S(1)} %get-tuple-element.108), channel_id=1, source_target_pairs={{0,4},{4,0},{8,12},{12,8},{16,20},{20,16},{24,28},{28,24},{1,5},{5... | collective-permute-start | bytes 1572872 | tf_op jit(solution)/shard_map/ppermute | solution.py:243
  235.0 43.6 %collective-permute-start.26 = (bf16[128,2048]{1,0:T(8,128)(2,1)S(1)}, bf16[128,2048]{1,0:T(8,128)(2,1)S(1)}, u32[]{:S(2)}, u32[]{:S(2)}) collective-permute-start(bf16[128,2048]{1,0:T(8,128)(2,1)S(1)} %fusion.74), channel_id=1, source_target_pairs={{0,24},{4,28},{8,0},{12,4},{16,8},{20,12},{24,16},{28,20},{1,25},{... | collective-permute-start | bytes 1572872 | tf_op jit(solution)/shard_map/ppermute | solution.py:248
  240.4 67.7 %collective-permute-start.56 = (bf16[128,2048]{1,0:T(8,128)(2,1)S(1)}, bf16[128,2048]{1,0:T(8,128)(2,1)S(1)}, u32[]{:S(2)}, u32[]{:S(2)}) collective-permute-start(bf16[128,2048]{1,0:T(8,128)(2,1)S(1)} %get-tuple-element.78), channel_id=1, source_target_pairs={{0,4},{4,0},{8,12},{12,8},{16,20},{20,16},{24,28},{28,24},{1,5},{5... | collective-permute-start | bytes 1572872 | tf_op jit(solution)/shard_map/ppermute | solution.py:243
  251.8 79.2 %collective-permute-start.42 = (bf16[2048,512]{1,0:T(8,128)(2,1)S(1)}, bf16[2048,512]{1,0:T(8,128)(2,1)S(1)}, u32[]{:S(2)}, u32[]{:S(2)}) collective-permute-start(bf16[2048,512]{1,0:T(8,128)(2,1)S(1)} %constant_dynamic-update-slice_fusion.40), channel_id=1, source_target_pairs={{0,1},{1,0},{2,3},{3,2},{4,5},{5,4},{6,7},{7,6},{8,9},{9,8},{10,11... | collective-permute-start | bytes 6291464 | tf_op jit(solution)/shard_map/ppermute | solution.py:235
  251.9 38.4 %collective-permute-start.54 = (bf16[128,2048]{1,0:T(8,128)(2,1)S(1)}, bf16[128,2048]{1,0:T(8,128)(2,1)S(1)}, u32[]{:S(2)}, u32[]{:S(2)}) collective-permute-start(bf16[128,2048]{1,0:T(8,128)(2,1)S(1)} %collective-permute-done.53), channel_id=1, source_target_pairs={{0,8},{4,12},{8,16},{12,20},{16,24},{20,28},{24,0},{28,4},{1,9},{5... | collective-permute-start | bytes 1572872 | tf_op jit(solution)/shard_map/ppermute | solution.py:248
  309.1 74.1 %collective-permute-start.43 = (bf16[256,2048]{1,0:T(8,128)(2,1)S(1)}, bf16[256,2048]{1,0:T(8,128)(2,1)S(1)}, u32[]{:S(2)}, u32[]{:S(2)}) collective-permute-start(bf16[256,2048]{1,0:T(8,128)(2,1)S(1)} %convert_element_type.358), channel_id=1, source_target_pairs={{0,1},{1,0},{2,3},{3,2},{4,5},{5,4},{6,7},{7,6},{8,9},{9,8},{10,11... | collective-permute-start | bytes 3145736 | tf_op jit(solution)/shard_map/ppermute | solution.py:235
  399.3 60.3 %collective-permute-start.60 = (bf16[128,2048]{1,0:T(8,128)(2,1)}, bf16[128,2048]{1,0:T(8,128)(2,1)S(1)}, u32[]{:S(2)}, u32[]{:S(2)}) collective-permute-start(bf16[128,2048]{1,0:T(8,128)(2,1)} %get-tuple-element.91), channel_id=1, source_target_pairs={{0,4},{4,0},{8,12},{12,8},{16,20},{20,16},{24,28},{28,24},{1,5},{5... | collective-permute-start | bytes 1572872 | tf_op jit(solution)/shard_map/ppermute | solution.py:243
  425.8 42.5 %collective-permute-start.46 = (bf16[128,2048]{1,0:T(8,128)(2,1)S(1)}, bf16[128,2048]{1,0:T(8,128)(2,1)S(1)}, u32[]{:S(2)}, u32[]{:S(2)}) collective-permute-start(bf16[128,2048]{1,0:T(8,128)(2,1)S(1)} %get-tuple-element.98), channel_id=1, source_target_pairs={{0,4},{4,0},{8,12},{12,8},{16,20},{20,16},{24,28},{28,24},{1,5},{5... | collective-permute-start | bytes 1572872 | tf_op jit(solution)/shard_map/ppermute | solution.py:243
  451.2 73.7 %collective-permute-start.97 = (f32[2048,512]{1,0:T(8,128)}, f32[2048,512]{1,0:T(8,128)}, u32[]{:S(2)}, u32[]{:S(2)}) collective-permute-start(f32[2048,512]{1,0:T(8,128)} %fusion.81), channel_id=1, source_target_pairs={{0,1},{1,0},{2,3},{3,2},{4,5},{5,4},{6,7},{7,6},{8,9},{9,8},{10,11... | collective-permute-start | bytes 12582920 | tf_op jit(solution)/shard_map/ppermute | solution.py:235
  468.4 40.5 %collective-permute-start.44 = (bf16[128,2048]{1,0:T(8,128)(2,1)}, bf16[128,2048]{1,0:T(8,128)(2,1)}, u32[]{:S(2)}, u32[]{:S(2)}) collective-permute-start(bf16[128,2048]{1,0:T(8,128)(2,1)} %get-tuple-element.96), channel_id=1, source_target_pairs={{0,4},{4,0},{8,12},{12,8},{16,20},{20,16},{24,28},{28,24},{1,5},{5... | collective-permute-start | bytes 1572872 | tf_op jit(solution)/shard_map/ppermute | solution.py:243
  646.3 60.3 %collective-permute-start.51 = (bf16[128,2048]{1,0:T(8,128)(2,1)}, bf16[128,2048]{1,0:T(8,128)(2,1)}, u32[]{:S(2)}, u32[]{:S(2)}) collective-permute-start(bf16[128,2048]{1,0:T(8,128)(2,1)} %fusion.66), channel_id=1, source_target_pairs={{0,2},{1,3},{2,0},{3,1},{4,6},{5,7},{6,4},{7,5},{8,10},{9,11},{10,... | collective-permute-start | bytes 1572872 | tf_op jit(solution)/shard_map/ppermute | solution.py:239
  648.8 40.9 %collective-permute-start.77 = (bf16[128,2048]{1,0:T(8,128)(2,1)}, bf16[128,2048]{1,0:T(8,128)(2,1)}, u32[]{:S(2)}, u32[]{:S(2)}) collective-permute-start(bf16[128,2048]{1,0:T(8,128)(2,1)} %get-tuple-element.87), channel_id=1, source_target_pairs={{0,4},{4,0},{8,12},{12,8},{16,20},{20,16},{24,28},{28,24},{1,5},{5... | collective-permute-start | bytes 1572872 | tf_op jit(solution)/shard_map/ppermute | solution.py:243
  651.7 44.0 %collective-permute-start.96 = (bf16[64,2048]{1,0:T(8,128)(2,1)}, bf16[64,2048]{1,0:T(8,128)(2,1)}, u32[]{:S(2)}, u32[]{:S(2)}) collective-permute-start(bf16[64,2048]{1,0:T(8,128)(2,1)} %add_convert_fusion.2), channel_id=1, source_target_pairs={{0,0},{16,1},{2,2},{18,3},{1,4},{17,5},{3,6},{19,7},{4,8},{20,9},{... | collective-permute-start | bytes 786440 | tf_op jit(solution)/shard_map/ppermute | solution.py:443
  710.9 76.3 %collective-permute-start.52 = (bf16[128,2048]{1,0:T(8,128)(2,1)}, bf16[128,2048]{1,0:T(8,128)(2,1)}, u32[]{:S(2)}, u32[]{:S(2)}) collective-permute-start(bf16[128,2048]{1,0:T(8,128)(2,1)} %get-tuple-element.130), channel_id=1, source_target_pairs={{0,1},{1,0},{2,3},{3,2},{4,5},{5,4},{6,7},{7,6},{8,9},{9,8},{10,11... | collective-permute-start | bytes 1572872 | tf_op jit(solution)/shard_map/ppermute | solution.py:235
  711.0 79.2 %collective-permute-start.85 = (f32[128,2048]{1,0:T(8,128)}, f32[128,2048]{1,0:T(8,128)}, u32[]{:S(2)}, u32[]{:S(2)}) collective-permute-start(f32[128,2048]{1,0:T(8,128)} %get-tuple-element.129), channel_id=1, source_target_pairs={{0,1},{1,0},{2,3},{3,2},{4,5},{5,4},{6,7},{7,6},{8,9},{9,8},{10,11... | collective-permute-start | bytes 3145736 | tf_op jit(solution)/shard_map/ppermute | solution.py:235
  (145 other events, 3118.9 us)
